TPU v7x, 32 devices: a whole 2x2x4 slice. The times are simulated.
32 devices in a mesh: ctx: 4 (over y, x), head: 8 (over z, core).
Axes of the slice: x: 2, y: 2, z: 4, core: 2. Of those that a mesh axis runs over, the one named last changes fastest.
Arguments:
- queries: bfloat16 [1024, 64, 128], P('ctx', 'head'), may hold values from -2 to 2
- keys: bfloat16 [1024, 64, 128], P('ctx', 'head'), may hold values from -2 to 2
- values: bfloat16 [1024, 64, 128], P('ctx', 'head'), may hold values from -2 to 2
- out_weight: bfloat16 [8192, 6144], P('head'), may hold values from -0.0625 to 0.0625
- decay_rate: float32 [64], P('head'), may hold values from 1.953125e-05 to 0.04
- out_grad: bfloat16 [1024, 6144], P(('ctx', 'head')), may hold values from -4 to 4
Outputs:
- layer_out: bfloat16 [1024, 6144], P(('ctx', 'head'))
- query_grad: bfloat16 [1024, 64, 128], P('ctx', 'head')
- key_grad: bfloat16 [1024, 64, 128], P('ctx', 'head')
- value_grad: bfloat16 [1024, 64, 128], P('ctx', 'head')
- weight_grad: float32 [8192, 6144], P('head', 'ctx')
All inputs are finite; a program needn't handle non-finite values.
Results may differ from a plain program's by a relative error of at most 0.0057.
Values may be sent and summed in bfloat16 or wider, within the bound.
A program may use at most 128 MiB of HBM per device.

v0:
```python
import jax
import jax.numpy as jnp
from jax import lax
from jax.sharding import PartitionSpec as P

precise_mode = lax.Precision.HIGHEST


def body(queries, keys, values, out_weight, decay_rate, out_grad):
    length = queries.shape[0]
    heads_here = queries.shape[1]
    head_size = queries.shape[2]
    places = jnp.arange(length, dtype=jnp.float32)
    offsets = places[:, None] - places[None, :]
    mask_decay = jnp.where(
        offsets[None] >= 0,
        jnp.exp(-decay_rate[:, None, None] * jnp.maximum(offsets, 0.0)[None]),
        0.0,
    )
    end_weight = jnp.exp(-decay_rate[None, :] * (length - 1.0 - places)[:, None])
    start_weight = jnp.exp(-decay_rate[None, :] * places[:, None])
    inner_weight = jnp.exp(-decay_rate[None, :] * (places + 1.0)[:, None])
    tail_weight = jnp.exp(-decay_rate[None, :] * (length - places)[:, None])
    shard_index = lax.axis_index("ctx")
    scores = jnp.einsum("thd,shd->hts", queries, keys, preferred_element_type=jnp.float32)
    attn = (scores * mask_decay).astype(jnp.bfloat16)
    inside = jnp.einsum("hts,she->the", attn, values, preferred_element_type=jnp.float32)
    keys_end = (keys * end_weight[:, :, None]).astype(jnp.bfloat16)
    block_state = jnp.einsum("thd,the->hde", keys_end, values, preferred_element_type=jnp.float32)
    piece = lax.all_gather(block_state[None], "ctx", axis=0, tiled=True)
    sources = jnp.arange(piece.shape[0], dtype=jnp.int32)
    gaps = (shard_index - 1 - sources).astype(jnp.float32)
    weights = jnp.where(
        (sources < shard_index)[:, None],
        jnp.exp(-decay_rate[None, :] * length * jnp.maximum(gaps, 0.0)[:, None]),
        0.0,
    )
    prev_state = jnp.einsum("jh,jhde->hde", weights, piece, precision=precise_mode)
    query_wide = queries.astype(jnp.float32)
    outside = inner_weight[:, :, None] * jnp.einsum(
        "thd,hde->the", query_wide, prev_state, precision=precise_mode
    )
    attn_out = (inside + outside).astype(jnp.bfloat16)
    flat_out = attn_out.reshape(length, heads_here * head_size)
    picked = flat_out
    layer_out = lax.psum_scatter(
        jnp.dot(picked, out_weight, preferred_element_type=jnp.float32),
        "head",
        scatter_dimension=0,
        tiled=True,
    ).astype(jnp.bfloat16)
    piece = lax.all_gather(out_grad, "head", axis=0, tiled=True)
    grad_part = lax.dot_general(
        piece, out_weight, (((1,), (1,)), ((), ())), preferred_element_type=jnp.float32
    )
    picked = flat_out
    weight_part = lax.dot_general(
        picked, piece, (((0,), (0,)), ((), ())), preferred_element_type=jnp.float32
    )
    grad_flat, weight_part = (grad_part, weight_part)
    weight_grad = lax.psum_scatter(weight_part, "ctx", scatter_dimension=1, tiled=True)
    grad_attn = grad_flat.astype(jnp.bfloat16).reshape(length, heads_here, head_size)
    queries_start = (queries * start_weight[:, :, None]).astype(jnp.bfloat16)
    grad_block = jnp.einsum(
        "thd,the->hde", queries_start, grad_attn, preferred_element_type=jnp.float32
    )
    piece = lax.all_gather(grad_block[None], "ctx", axis=0, tiled=True)
    sources = jnp.arange(piece.shape[0], dtype=jnp.int32)
    gaps = (sources - shard_index - 1).astype(jnp.float32)
    weights = jnp.where(
        (sources > shard_index)[:, None],
        jnp.exp(-decay_rate[None, :] * length * jnp.maximum(gaps, 0.0)[:, None]),
        0.0,
    )
    next_grad = jnp.einsum("jh,jhde->hde", weights, piece, precision=precise_mode)
    grad_wide = grad_attn.astype(jnp.float32)
    value_wide = values.astype(jnp.float32)
    key_wide = keys.astype(jnp.float32)
    grad_scores = (
        jnp.einsum("the,she->hts", grad_attn, values, preferred_element_type=jnp.float32)
        * mask_decay
    ).astype(jnp.bfloat16)
    query_grad = jnp.einsum(
        "hts,shd->thd", grad_scores, keys, preferred_element_type=jnp.float32
    ) + inner_weight[:, :, None] * jnp.einsum(
        "the,hde->thd", grad_wide, prev_state, precision=precise_mode
    )
    key_grad = jnp.einsum(
        "hts,thd->shd", grad_scores, queries, preferred_element_type=jnp.float32
    ) + tail_weight[:, :, None] * jnp.einsum(
        "she,hde->shd", value_wide, next_grad, precision=precise_mode
    )
    value_grad = jnp.einsum(
        "hts,the->she", attn, grad_attn, preferred_element_type=jnp.float32
    ) + tail_weight[:, :, None] * jnp.einsum(
        "shd,hde->she", key_wide, next_grad, precision=precise_mode
    )
    return (
        layer_out,
        query_grad.astype(jnp.bfloat16),
        key_grad.astype(jnp.bfloat16),
        value_grad.astype(jnp.bfloat16),
        weight_grad,
    )


def solution(mesh):
    return jax.shard_map(
        body,
        mesh=mesh,
        in_specs=(
            P("ctx", "head", None),
            P("ctx", "head", None),
            P("ctx", "head", None),
            P("head", None),
            P("head"),
            P(("ctx", "head"), None),
        ),
        out_specs=(
            P(("ctx", "head"), None),
            P("ctx", "head", None),
            P("ctx", "head", None),
            P("ctx", "head", None),
            P("head", "ctx"),
        ),
        check_vma=False,
    )
```

profile of v0, /device:TPU:0, one launch (start us, length us, event | category | flops | bytes accessed | tf_op | source)
XLA Modules:
  0.0 427.0 jit_solution(17294447304867530970)
XLA Ops:
  7.2 0.7 all-gather.6.cloned.1.call-update
  8.0 0.7 broadcast_multiply_fusion
  8.9 1.4 multiply_convert_fusion.3
  10.3 1.1 fusion.16
  11.6 0.3 multiply_convert_fusion.2
  12.0 38.6 %all-gather.6.cloned.1.call-done = bf16[256,6144]{1,0:T(8,128)(2,1)} async-done(((bf16[32,6144]{1,0:T(8,128)(2,1)}), bf16[256,6144]{1,0:T(8,128)(2,1)}) %all-gather.6.cloned.1.call-update) | async-done | bytes 3145744 | tf_op jit(solution)/shard_map/all_gather | solution.py:52
  50.6 9.0 %convolution_convert_fusion = bf16[256,1024]{1,0:T(8,128)(2,1)S(1)} fusion(bf16[256,6144]{1,0:T(8,128)(2,1)} %all-gather.6.cloned.1.call-done, bf16[1024,6144]{1,0:T(8,128)(2,1)} %param.9), kind=kOutput, calls=%fused_computation.26 | convolution fusion | flops 3221487616 | bytes 16252928 | tf_op jit(solution)/shard_map/dot_general | solution.py:53
  59.8 1.1 fusion.14
  61.6 0.6 multiply_convert_fusion.1
  62.2 1.0 copy-done.3
  63.2 1.4 convolution_bitcast_fusion.7
  64.7 22.5 %all-gather.8.cloned.1.call-done = f32[32,128,128]{2,1,0:T(8,128)} async-done(((f32[8,128,128]{2,1,0:T(8,128)}), f32[32,128,128]{2,1,0:T(8,128)}) %all-gather.8.cloned.1.call-update) | async-done | bytes 2097168 | tf_op jit(solution)/shard_map/all_gather | solution.py:30
  87.1 6.7 %fusion = f32[8,1,128,128]{3,1,2,0:T(1,128)S(1)} fusion(f32[4,8,1,1]{0,2,3,1:T(1,128)S(1)} %copy.67, f32[4,8,128,128]{3,2,1,0:T(8,128)} %bitcast.79), kind=kOutput, calls=%fused_computation.1 | convolution fusion | flops 6291456 | bytes 2621568 | tf_op jit(solution)/shard_map/jh,jhde->hde/dot_general | solution.py:38
  93.8 0.7 fusion.10
  94.5 10.7 %fusion.30 = f32[256,6144]{1,0:T(8,128)} fusion(bf16[256,1024]{0,1:T(8,128)(2,1)S(1)} %bitcast.75, bf16[1024,6144]{1,0:T(8,128)(2,1)} %param.9), kind=kOutput, calls=%fused_computation.60 | convolution fusion | flops 3221225472 | bytes 19398656 | tf_op jit(solution)/shard_map/dot_general | solution.py:47
  105.2 0.3 reduce-scatter.5.cloned.1.call-start
  105.5 12.0 %fusion.31 = f32[1024,6144]{1,0:T(8,128)} fusion(bf16[256,1024]{0,1:T(8,128)(2,1)S(1)} %bitcast.76, bf16[256,6144]{1,0:T(8,128)(2,1)} %all-gather.6.cloned.1.call-done), kind=kOutput, calls=%fused_computation.61 | convolution fusion | flops 3221225472 | bytes 28835840 | tf_op jit(solution)/shard_map/dot_general | solution.py:57
  117.5 0.7 multiply_convert_fusion
  118.2 1.0 copy-done.4
  119.2 0.5 convolution_bitcast_fusion.6
  119.7 0.6 fusion.11
  120.3 1.1 copy.64
  121.4 2.8 convolution_bitcast_fusion.4
  124.2 0.5 convolution_bitcast_fusion.5
  124.8 1.9 multiply_reduce_fusion
  126.7 0.7 fusion.13
  127.4 1.1 copy.66
  128.6 0.6 fusion.12
  129.2 1.1 copy.65
  130.3 66.4 %reduce-scatter.3.cloned.1.call-done = f32[32,6144]{1,0:T(8,128)} async-done(((f32[256,6144]{1,0:T(8,128)}), f32[32,6144]{1,0:T(8,128)}) %reduce-scatter.3.cloned.1.call-update) | async-done | bytes 786448 | tf_op jit(solution)/shard_map/reduce_scatter | solution.py:46
  196.7 1.9 convert_element_type.59
  198.6 221.8 %reduce-scatter.5.cloned.1.call-done = f32[1024,1536]{1,0:T(8,128)} async-done(((f32[1024,6144]{1,0:T(8,128)}), f32[1024,1536]{1,0:T(8,128)}) %reduce-scatter.5.cloned.1.call-update) | async-done | bytes 6291472 | tf_op jit(solution)/shard_map/reduce_scatter | solution.py:61
  (35 shorter events, 1.4 us)
Async XLA Ops:
  7.2 3.1 copy-start
  7.2 4.4 %copy-start.1 = (bf16[256,8,128]{2,1,0:T(8,128)(2,1)S(1)}, bf16[256,8,128]{2,1,0:T(8,128)(2,1)}, u32[]{:S(2)}) copy-start(bf16[256,8,128]{2,1,0:T(8,128)(2,1)} %param.6) | copy-start | bytes 1572868
  7.2 43.4 %all-gather.6.cloned.1.call-start = ((), (), s32[]{:S(2)}) async-start(), calls=%async_computation.3 | async-start | bytes 3538944 | tf_op jit(solution)/shard_map/all_gather | solution.py:52
  7.9 79.2 %all-gather.8.cloned.1.call-start = ((), (), s32[]{:S(2)}) async-start(), calls=%async_computation.5 | async-start | bytes 2621440 | tf_op jit(solution)/shard_map/all_gather | solution.py:30
  11.4 113.3 %all-gather.10.cloned.1.call-start = ((), (), s32[]{:S(2)}) async-start(), calls=%async_computation.6 | async-start | bytes 2621440 | tf_op jit(solution)/shard_map/all_gather | solution.py:67
  59.6 2.0 copy-start.2
  61.0 135.7 %reduce-scatter.3.cloned.1.call-start = ((), (), s32[]{:S(2)}) async-start(), calls=%async_computation.2 | async-start | bytes 7077888 | tf_op jit(solution)/shard_map/reduce_scatter | solution.py:46
  62.2 1.0 copy-start.3
  87.1 6.7 %copy-start.7 = (f32[256,8,128]{0,2,1:T(8,128)S(1)}, f32[256,8,128]{0,2,1:T(8,128)}, u32[]{:S(2)}) copy-start(f32[256,8,128]{0,2,1:T(8,128)} %convolution_bitcast_fusion.7) | copy-start | bytes 3145732
  105.2 315.2 %reduce-scatter.5.cloned.1.call-start = ((), (), s32[]{:S(2)}) async-start(), calls=%async_computation.4 | async-start | bytes 31457280 | tf_op jit(solution)/shard_map/reduce_scatter | solution.py:61
  118.2 1.0 copy-start.4
  121.4 2.8 copy-start.5
  124.8 2.0 copy-start.6
Sparse Core Ops, SparseCore 0:
  9.6 40.9 all-gather.5
  53.0 34.0 all-gather.7
  89.6 35.1 all-gather.9
  126.9 69.7 reduce-scatter.2
  200.2 220.1 reduce-scatter.4
where the time goes:
time: 427 us
  waiting for transfers between devices  350 us (82%)
  matrix products  49.7 us (12%)
  between operations  14 us (3%)
  other arithmetic  6.57 us (2%)
  local copies, waits for them, and re-layouts  5.91 us (1%)
    reduce_scatter x1, waiting for transfers between devices, body(): lax.psum_scatter(weight_part, 'ctx', scatter_dimension=1, tiled=True)  222 us
    reduce_scatter x1, waiting for transfers between devices, body(): lax.psum_scatter(jnp.dot(picked, out_weight, preferred_element_type=jnp.f...  66.4 us
    all_gather x1, waiting for transfers between devices, body(): piece = lax.all_gather(out_grad, 'head', axis=0, tiled=True)  38.6 us
    all_gather x1, waiting for transfers between devices, body(): piece = lax.all_gather(block_state[None], 'ctx', axis=0, tiled=True)  22.5 us
    dot_general x1, matrix products, body(): lax.dot_general(picked, piece, (((0,), (0,)), ((), ())), preferred_elemen...  12 us
    dot_general x1, matrix products, body(): jnp.dot(picked, out_weight, preferred_element_type=jnp.float32)  10.7 us
    dot_general x1, matrix products, body(): lax.dot_general(piece, out_weight, (((1,), (1,)), ((), ())), preferred_el...  8.97 us
  transfers between devices with their start and end apart: 5, of which 5 were waited for; matrix products, arithmetic and copies ran while one was open for 14% of the time, Pallas kernels for 0%

commit v1 on v0

--- a/solution.py
+++ b/solution.py
@@ -27,7 +27,12 @@
     inside = jnp.einsum("hts,she->the", attn, values, preferred_element_type=jnp.float32)
     keys_end = (keys * end_weight[:, :, None]).astype(jnp.bfloat16)
     block_state = jnp.einsum("thd,the->hde", keys_end, values, preferred_element_type=jnp.float32)
-    piece = lax.all_gather(block_state[None], "ctx", axis=0, tiled=True)
+    ring = [block_state[None]]
+    for hop in range(3):
+        ring.append(lax.ppermute(ring[-1], "ctx", [(dev, (dev + 1) % 4) for dev in range(4)]))
+    piece = jnp.roll(
+        jnp.concatenate(ring[::-1], axis=0), (lax.axis_index("ctx") + 1) * ring[0].shape[0], axis=0
+    )
     sources = jnp.arange(piece.shape[0], dtype=jnp.int32)
     gaps = (shard_index - 1 - sources).astype(jnp.float32)
     weights = jnp.where(

time: 427 us -> 400 us (0.937)
  waiting for transfers between devices: 350 us -> 310 us
  local copies, waits for them, and re-layouts: 5.91 us -> 11.6 us
    all_gather x1, waiting for transfers between devices: 38.6 us -> 9.37 us  [body(): piece = lax.all_gather(out_grad, 'head', axis=0, tiled=True)]
    all_gather x1 -> x0, waiting for transfers between devices: 22.5 us -> none  [body(): piece = lax.all_gather(block_state[None], 'ctx', axis=0, tiled=True)]
    ppermute x0 -> x3, waiting for transfers between devices: none -> 22.3 us  [body(): lax.ppermute(ring[-1], 'ctx', [(dev, (dev + 1) % 4) for dev in range(4)])]
    reduce_scatter x1, waiting for transfers between devices: 66.4 us -> 55.9 us  [body(): lax.psum_scatter(jnp.dot(picked, out_weight, preferred_element_type=jnp.f...]
    unnamed x19 -> x40, local copies, waits for them, and re-layouts: 5.38 us -> 9.71 us
  transfers between devices with their start and end apart: 5 -> 7, of which waited for: 5 -> 5; matrix products, arithmetic and copies ran while one was open for 14% -> 17% of each run, Pallas kernels for 0% -> 0%
where the time goes in v1:
time: 400 us; the launch traced here: 399 us
  waiting for transfers between devices  310 us (78%)
  matrix products  51.2 us (13%)
  between operations  14.1 us (4%)
  local copies, waits for them, and re-layouts  11.6 us (3%)
  other arithmetic  8.08 us (2%)
  starting transfers between devices  4.36 us (1%)
    reduce_scatter x1, waiting for transfers between devices, body(): lax.psum_scatter(weight_part, 'ctx', scatter_dimension=1, tiled=True)  222 us
    reduce_scatter x1, waiting for transfers between devices, body(): lax.psum_scatter(jnp.dot(picked, out_weight, preferred_element_type=jnp.f...  55.9 us
    ppermute x3, waiting for transfers between devices, body(): lax.ppermute(ring[-1], 'ctx', [(dev, (dev + 1) % 4) for dev in range(4)])  22.3 us
    dot_general x1, matrix products, body(): lax.dot_general(picked, piece, (((0,), (0,)), ((), ())), preferred_elemen...  12 us
    dot_general x1, matrix products, body(): jnp.dot(picked, out_weight, preferred_element_type=jnp.float32)  10.1 us
    dot_general x1, matrix products, body(): lax.dot_general(piece, out_weight, (((1,), (1,)), ((), ())), preferred_el...  9.77 us
    unnamed x40, local copies, waits for them, and re-layouts  9.71 us
    all_gather x1, waiting for transfers between devices, body(): piece = lax.all_gather(out_grad, 'head', axis=0, tiled=True)  9.37 us
  transfers between devices with their start and end apart: 7, of which 5 were waited for; matrix products, arithmetic and copies ran while one was open for 17% of the time, Pallas kernels for 0%

profile of v1, /device:TPU:0, one launch (start us, length us, event | category | flops | bytes accessed | tf_op | source)
XLA Modules:
  0.0 399.4 jit_solution(13873878071291659494)
XLA Ops:
  8.0 1.2 broadcast_multiply_fusion
  9.4 1.4 multiply_convert_fusion.3
  11.1 3.0 collective-permute-start
  15.6 11.5 %collective-permute-done = f32[1,8,128,128]{3,2,1,0:T(8,128)S(1)} collective-permute-done((f32[1,8,128,128]{3,2,1,0:T(8,128)S(1)}, f32[1,8,128,128]{3,2,1,0:T(8,128)S(1)}, u32[]{:S(2)}, u32[]{:S(2)}) %collective-permute-start) | collective-permute-done | bytes 524320 | tf_op jit(solution)/shard_map/ppermute | solution.py:32
  27.0 0.8 collective-permute-start.1
  28.2 2.3 multiply_convert_fusion.1
  30.5 10.8 %collective-permute-done.1 = f32[1,8,128,128]{3,2,1,0:T(8,128)} collective-permute-done((f32[1,8,128,128]{3,2,1,0:T(8,128)S(1)}, f32[1,8,128,128]{3,2,1,0:T(8,128)}, u32[]{:S(2)}, u32[]{:S(2)}) %collective-permute-start.1) | collective-permute-done | bytes 524320 | tf_op jit(solution)/shard_map/ppermute | solution.py:32
  41.3 9.4 %all-gather.4.cloned.1.call-done = bf16[256,6144]{1,0:T(8,128)(2,1)} async-done(((bf16[32,6144]{1,0:T(8,128)(2,1)}), bf16[256,6144]{1,0:T(8,128)(2,1)}) %all-gather.4.cloned.1.call-update) | async-done | bytes 3145744 | tf_op jit(solution)/shard_map/all_gather | solution.py:57
  50.6 9.8 %convolution_convert_fusion = bf16[256,1024]{1,0:T(8,128)(2,1)} fusion(bf16[256,6144]{1,0:T(8,128)(2,1)} %all-gather.4.cloned.1.call-done, bf16[1024,6144]{1,0:T(8,128)(2,1)} %param.9), kind=kOutput, calls=%fused_computation.26 | convolution fusion | flops 3221487616 | bytes 16252928 | tf_op jit(solution)/shard_map/dot_general | solution.py:58
  60.4 1.2 copy.84
  61.6 1.1 fusion.14
  63.3 1.7 convolution_bitcast_fusion.7
  65.0 1.1 constant_dynamic-update-slice_fusion.7
  66.1 1.1 constant_dynamic-update-slice_fusion.6
  67.2 1.1 constant_dynamic-update-slice_fusion.3
  68.3 1.1 constant_dynamic-update-slice_fusion.2
  69.8 4.3 %fusion = f32[8,1,128,128]{3,1,2,0:T(1,128)S(1)} fusion(f32[4,8,1,1]{0,2,3,1:T(1,128)S(1)} %copy.67, f32[4,8,128,128]{3,2,1,0:T(8,128)S(1)} %constant_dynamic-slice_fusion), kind=kOutput, calls=%fused_computation.1 | convolution fusion | flops 6291456 | bytes 2621568 | tf_op jit(solution)/shard_map/jh,jhde->hde/dot_general | solution.py:43
  74.7 10.1 %fusion.29 = f32[256,6144]{1,0:T(8,128)} fusion(bf16[256,1024]{0,1:T(8,128)(2,1)S(1)} %bitcast.76, bf16[1024,6144]{1,0:T(8,128)(2,1)} %param.9), kind=kOutput, calls=%fused_computation.69 | convolution fusion | flops 3221225472 | bytes 19398656 | tf_op jit(solution)/shard_map/dot_general | solution.py:52
  85.1 12.0 %fusion.30 = f32[1024,6144]{1,0:T(8,128)} fusion(bf16[256,1024]{0,1:T(8,128)(2,1)S(1)} %bitcast.77, bf16[256,6144]{1,0:T(8,128)(2,1)} %all-gather.4.cloned.1.call-done), kind=kOutput, calls=%fused_computation.70 | convolution fusion | flops 3221225472 | bytes 28835840 | tf_op jit(solution)/shard_map/dot_general | solution.py:62
  97.1 0.8 copy-done.7
  98.0 0.7 multiply_convert_fusion
  98.7 1.0 copy-done.3
  100.8 1.1 copy.64
  101.9 2.7 convolution_bitcast_fusion.4
  104.6 2.0 convolution_bitcast_fusion.5
  106.6 1.9 multiply_reduce_fusion
  108.5 1.9 fusion.13
  110.3 1.1 copy.66
  112.1 1.1 copy.65
  113.3 55.9 %reduce-scatter.3.cloned.1.call-done = f32[32,6144]{1,0:T(8,128)} async-done(((f32[256,6144]{1,0:T(8,128)}), f32[32,6144]{1,0:T(8,128)}) %reduce-scatter.3.cloned.1.call-update) | async-done | bytes 786448 | tf_op jit(solution)/shard_map/reduce_scatter | solution.py:51
  169.1 1.9 convert_element_type.59
  171.0 221.8 %reduce-scatter.5.cloned.1.call-done = f32[1024,1536]{1,0:T(8,128)} async-done(((f32[1024,6144]{1,0:T(8,128)}), f32[1024,1536]{1,0:T(8,128)}) %reduce-scatter.5.cloned.1.call-update) | async-done | bytes 6291472 | tf_op jit(solution)/shard_map/reduce_scatter | solution.py:66
  (61 shorter events, 6.6 us)
Async XLA Ops:
  7.2 3.6 copy-start
  7.2 21.0 %copy-start.2 = (bf16[256,8,128]{2,1,0:T(8,128)(2,1)S(1)}, bf16[256,8,128]{2,1,0:T(8,128)(2,1)}, u32[]{:S(2)}) copy-start(bf16[256,8,128]{2,1,0:T(8,128)(2,1)} %param.7) | copy-start | bytes 1572868
  7.2 20.6 %copy-start.1 = (bf16[256,8,128]{2,1,0:T(8,128)(2,1)S(1)}, bf16[256,8,128]{2,1,0:T(8,128)(2,1)}, u32[]{:S(2)}) copy-start(bf16[256,8,128]{2,1,0:T(8,128)(2,1)} %param.6) | copy-start | bytes 1572868
  7.2 43.4 %all-gather.4.cloned.1.call-start = ((), (), s32[]{:S(2)}) async-start(), calls=%async_computation.3 | async-start | bytes 3538944 | tf_op jit(solution)/shard_map/all_gather | solution.py:57
  7.9 98.7 %all-gather.6.cloned.1.call-start = ((), (), s32[]{:S(2)}) async-start(), calls=%async_computation.5 | async-start | bytes 2621440 | tf_op jit(solution)/shard_map/all_gather | solution.py:72
  9.2 6.2 %copy-start.10 = (f32[8]{0:T(128)}, f32[8]{0:T(128)S(1)}, u32[]{:S(2)}) copy-start(f32[8]{0:T(128)S(1)} %get-tuple-element.22) | copy-start | bytes 100
  11.1 15.9 %collective-permute-start = (f32[1,8,128,128]{3,2,1,0:T(8,128)S(1)}, f32[1,8,128,128]{3,2,1,0:T(8,128)S(1)}, u32[]{:S(2)}, u32[]{:S(2)}) collective-permute-start(f32[1,8,128,128]{3,2,1,0:T(8,128)S(1)} %convolution_bitcast_fusion.8), channel_id=1, source_target_pairs={{0,8},{8,16},{16,24},{24,0},{1,9},{9,17},{17,25},{25,1},{2,10},{10... | collective-permute-start | bytes 1572872 | tf_op jit(solution)/shard_map/ppermute | solution.py:32
  15.5 25.8 %copy-start.6 = (pred[256,256]{1,0:T(8,128)(4,1)}, pred[256,256]{1,0:T(8,128)(4,1)S(1)}, u32[]{:S(2)}) copy-start(pred[256,256]{1,0:T(8,128)(4,1)S(1)} %fusion.28) | copy-start | bytes 196612
  27.0 23.6 %copy-start.4 = (f32[1,8,128,128]{3,2,1,0:T(8,128)}, f32[1,8,128,128]{3,2,1,0:T(8,128)S(1)}, u32[]{:S(2)}) copy-start(f32[1,8,128,128]{3,2,1,0:T(8,128)S(1)} %collective-permute-done) | copy-start | bytes 1572868
  27.0 14.2 %collective-permute-start.1 = (f32[1,8,128,128]{3,2,1,0:T(8,128)S(1)}, f32[1,8,128,128]{3,2,1,0:T(8,128)}, u32[]{:S(2)}, u32[]{:S(2)}) collective-permute-start(f32[1,8,128,128]{3,2,1,0:T(8,128)S(1)} %collective-permute-done), channel_id=1, source_target_pairs={{0,8},{8,16},{16,24},{24,0},{1,9},{9,17},{17,25},{25,1},{2,10},{10... | collective-permute-start | bytes 1572872 | tf_op jit(solution)/shard_map/ppermute | solution.py:32
  30.4 32.6 %copy-start.8 = (f32[4]{0:T(128)S(1)}, f32[4]{0:T(128)}, u32[]{:S(2)}) copy-start(f32[4]{0:T(128)} %get-tuple-element.25) | copy-start | bytes 52
  30.5 32.6 %copy-start.9 = (f32[4]{0:T(128)S(1)}, f32[4]{0:T(128)}, u32[]{:S(2)}) copy-start(f32[4]{0:T(128)} %get-tuple-element.26) | copy-start | bytes 52
  30.5 32.6 %copy-start.12 = (f32[8]{0:T(128)S(1)}, f32[8]{0:T(128)}, u32[]{:S(2)}) copy-start(f32[8]{0:T(128)} %get-tuple-element.21) | copy-start | bytes 100
  30.5 32.6 %copy-start.13 = (pred[4]{0:T(512)(128)(4,1)S(1)}, pred[4]{0:T(512)(128)(4,1)}, u32[]{:S(2)}) copy-start(pred[4]{0:T(512)(128)(4,1)} %get-tuple-element.23) | copy-start | bytes 16
  30.5 32.6 %copy-start.14 = (pred[4]{0:T(512)(128)(4,1)S(1)}, pred[4]{0:T(512)(128)(4,1)}, u32[]{:S(2)}) copy-start(pred[4]{0:T(512)(128)(4,1)} %get-tuple-element.24) | copy-start | bytes 16
  41.3 23.7 %collective-permute-start.2 = (f32[1,8,128,128]{3,2,1,0:T(8,128)}, f32[1,8,128,128]{3,2,1,0:T(8,128)}, u32[]{:S(2)}, u32[]{:S(2)}) collective-permute-start(f32[1,8,128,128]{3,2,1,0:T(8,128)} %collective-permute-done.1), channel_id=1, source_target_pairs={{0,8},{8,16},{16,24},{24,0},{1,9},{9,17},{17,25},{25,1},{2,10},{10... | collective-permute-start | bytes 1572872 | tf_op jit(solution)/shard_map/ppermute | solution.py:32
  62.8 4.4 %copy-start.5 = (f32[1,8,128,128]{3,2,1,0:T(8,128)S(1)}, f32[1,8,128,128]{3,2,1,0:T(8,128)}, u32[]{:S(2)}) copy-start(f32[1,8,128,128]{3,2,1,0:T(8,128)} %copy-done.4) | copy-start | bytes 1572868
  62.8 106.3 %reduce-scatter.3.cloned.1.call-start = ((), (), s32[]{:S(2)}) async-start(), calls=%async_computation.2 | async-start | bytes 7077888 | tf_op jit(solution)/shard_map/reduce_scatter | solution.py:51
  84.8 308.0 %reduce-scatter.5.cloned.1.call-start = ((), (), s32[]{:S(2)}) async-start(), calls=%async_computation.4 | async-start | bytes 31457280 | tf_op jit(solution)/shard_map/reduce_scatter | solution.py:66
  97.1 0.8 copy-start.7
  97.1 0.8 copy-start.11
  98.6 1.0 copy-start.3
Sparse Core Ops, SparseCore 0:
  9.7 40.9 all-gather.3
  62.9 34.0 all-gather.5
  99.4 69.7 reduce-scatter.2
  172.6 220.1 reduce-scatter.4
